TPU v7x, 32 devices: a whole 2x2x4 slice. The times are simulated.
32 devices in a mesh: seg: 8 (over z, core), seq: 4 (over y, x).
Axes of the slice: x: 2, y: 2, z: 4, core: 2. Of those that a mesh axis runs over, the one named last changes fastest.
Arguments:
- layer_input: bfloat16 [8, 2048, 1024], P('seg', 'seq'), may hold values from -6 to 6
- output_grad: bfloat16 [8, 2048, 1024], P('seg', 'seq'), may hold values from -6 to 6
- norm1_gain: float32 [1024], replicated, may hold values from 0.5 to 1.5
- norm2_gain: float32 [1024], replicated, may hold values from 0.5 to 1.5
- w_qkv: bfloat16 [1024, 3072], replicated, may hold values from -0.25 to 0.25
- w_out: bfloat16 [1024, 1024], replicated, may hold values from -0.75 to 0.75
- w_gate: bfloat16 [1024, 2816], replicated, may hold values from -0.1875 to 0.1875
- w_up: bfloat16 [1024, 2816], replicated, may hold values from -0.1875 to 0.1875
- w_down: bfloat16 [2816, 1024], replicated, may hold values from -0.109375 to 0.109375
- mem_keys: bfloat16 [8, 1024, 1024], P('seg', 'seq'), may hold values from -8 to 8
- mem_values: bfloat16 [8, 1024, 1024], P('seg', 'seq'), may hold values from -8 to 8
- memory_flags: int32 [8], replicated, may hold values from 0 to 1, as said below
- sources: int32 [8, 3], replicated, may hold values from 0 to 7, as said below
Outputs:
- output: bfloat16 [8, 2048, 1024], P('seg', 'seq')
- input_grad: float32 [8, 2048, 1024], P('seg', 'seq')
- grad_norm1: float32 [1024], P('seq')
- grad_norm2: float32 [1024], P('seq')
- grad_qkv: float32 [1024, 3072], P('seq')
- grad_out: float32 [1024, 1024], P('seq')
- grad_gate: float32 [1024, 2816], P('seq')
- grad_up: float32 [1024, 2816], P('seq')
- grad_down: float32 [2816, 1024], P('seq')
Inputs may be any that keep to these rules, and one draw needn't show every extreme that they name: `memory_flags`: exactly half of the segments have flag 1. `sources`: row s lists 3 different segments, none of them s. The first column is a permutation of the segments, and the first source of a segment has the other flag than the segment.
All inputs are finite; a program needn't handle non-finite values.
Results may differ from a plain program's by a relative error of at most 0.023.
Values may be sent and summed in bfloat16 or wider, within the bound.
A program may use at most 256 MiB of HBM per device.

v0:
```python
import jax
import jax.numpy as jnp
from jax import lax
from jax.sharding import PartitionSpec as P

D = 1024
HEADS = 8
HEAD_DIM = 128
masked_score = -1e30
epsilon = 1e-06
rotary_base = 10000.0


def product(former, latter):
    return jnp.dot(former, latter, preferred_element_type=jnp.float32)


def product_nt(former, latter):
    return lax.dot_general(
        former, latter, (((1,), (1,)), ((), ())), preferred_element_type=jnp.float32
    )


def product_tn(former, latter):
    return lax.dot_general(
        former, latter, (((0,), (0,)), ((), ())), preferred_element_type=jnp.float32
    )


def norm_forward(values, norm_gain):
    inverse = lax.rsqrt(jnp.mean(values * values, axis=-1, keepdims=True) + epsilon)
    return (values * inverse * norm_gain, inverse)


def norm_backward(values, inverse, norm_gain, upstream):
    weighted = upstream * norm_gain
    inner_mean = jnp.mean(weighted * values, axis=-1, keepdims=True)
    grad_values = inverse * weighted - inverse * inverse * inverse * values * inner_mean
    grad_gain = jnp.sum(upstream * values * inverse, axis=0)
    return (grad_values, grad_gain)


def turn_tables(positions):
    half_dim = HEAD_DIM // 2
    exponent = -2.0 * jnp.arange(half_dim, dtype=jnp.float32) / HEAD_DIM
    angles = positions[:, None] * jnp.power(rotary_base, exponent)[None, :]
    angles = jnp.concatenate([angles, angles], axis=1)
    return (jnp.cos(angles)[:, None, :], jnp.sin(angles)[:, None, :])


def rotate(matrix, cosine_table, sine_table, direction):
    row_count = matrix.shape[0]
    half_dim = HEAD_DIM // 2
    shaped = matrix.reshape(row_count, HEADS, HEAD_DIM)
    turned = jnp.concatenate([-shaped[..., half_dim:], shaped[..., :half_dim]], axis=-1)
    return (shaped * cosine_table + direction * turned * sine_table).reshape(
        row_count, HEADS * HEAD_DIM
    )


def on_device(
    layer_input,
    output_grad,
    norm1_gain,
    norm2_gain,
    w_qkv,
    w_out,
    w_gate,
    w_up,
    w_down,
    mem_keys,
    mem_values,
    memory_flags,
    sources,
):
    seg_index = lax.axis_index("seg")
    seq_index = lax.axis_index("seq")
    tokens = layer_input.shape[1]
    score_scale = HEAD_DIM ** (-0.5)
    flag_on = lax.dynamic_index_in_dim(memory_flags, seg_index, 0, keepdims=False) > 0
    listed = lax.dynamic_index_in_dim(sources, seg_index, 0, keepdims=False)
    picked = jnp.concatenate([jnp.reshape(seg_index, (1,)), listed])
    every_keys, every_values = (
        lax.all_gather(mem_keys, "seg", axis=0, tiled=True),
        lax.all_gather(mem_values, "seg", axis=0, tiled=True),
    )
    chosen_keys = jnp.take(every_keys, picked, axis=0)
    chosen_values = jnp.take(every_values, picked, axis=0)
    memory_keys, memory_values = (
        lax.all_gather(chosen_keys, "seq", axis=1, tiled=True),
        lax.all_gather(chosen_values, "seq", axis=1, tiled=True),
    )
    memory_key_blocks = memory_keys.reshape(-1, tokens, HEADS, HEAD_DIM)
    memory_value_blocks = memory_values.reshape(-1, tokens, HEADS, HEAD_DIM)
    memory_blocks = memory_key_blocks.shape[0]
    inputs = layer_input[0].astype(jnp.float32)
    first_norm, first_inverse = norm_forward(inputs, norm1_gain)
    first_low = first_norm.astype(jnp.bfloat16)
    projected = product(first_low, w_qkv)
    positions = seq_index * tokens + lax.iota(jnp.int32, tokens)
    cosine_table, sine_table = turn_tables(positions.astype(jnp.float32))
    queries = rotate(projected[:, :D], cosine_table, sine_table, 1.0).astype(jnp.bfloat16)
    own_keys = rotate(projected[:, D : 2 * D], cosine_table, sine_table, 1.0).astype(jnp.bfloat16)
    own_values = projected[:, 2 * D :].astype(jnp.bfloat16)
    all_keys, all_values = (
        lax.all_gather(own_keys, "seq", axis=0, tiled=True),
        lax.all_gather(own_values, "seq", axis=0, tiled=True),
    )
    key_blocks = all_keys.reshape(-1, tokens, HEADS, HEAD_DIM)
    value_blocks = all_values.reshape(-1, tokens, HEADS, HEAD_DIM)
    query_heads = queries.reshape(tokens, HEADS, HEAD_DIM)
    memory_open = jnp.broadcast_to(flag_on, (tokens, tokens))
    own_count = seq_index + 1
    key_offsets = lax.iota(jnp.int32, tokens)

    def own_open(block):
        return (block * tokens + key_offsets)[None, :] <= positions[:, None]

    def block_scores(key_block, open_mask):
        raw = (
            jnp.einsum("qhd,khd->hqk", query_heads, key_block, preferred_element_type=jnp.float32)
            * score_scale
        )
        return jnp.where(open_mask[None], raw, masked_score)

    def sweep(step, carry):

        def memory_turn(block, state):
            return step(
                state,
                block,
                memory_key_blocks[block],
                memory_value_blocks[block],
                memory_open,
                False,
            )

        def own_turn(block, state):
            return step(state, block, key_blocks[block], value_blocks[block], own_open(block), True)

        carry = lax.fori_loop(0, memory_blocks, memory_turn, carry)
        return lax.fori_loop(0, own_count, own_turn, carry)

    def max_step(carry, block, key_block, value_block, open_mask, own):
        row_max, row_sum = carry
        scores = block_scores(key_block, open_mask)
        new_max = jnp.maximum(row_max, jnp.max(scores, axis=2))
        row_sum = row_sum * jnp.exp(row_max - new_max) + jnp.sum(
            jnp.exp(scores - new_max[..., None]), axis=2
        )
        return (new_max, row_sum)

    start_max = jnp.full((HEADS, tokens), masked_score, jnp.float32)
    row_max, row_sum = sweep(max_step, (start_max, jnp.zeros((HEADS, tokens), jnp.float32)))
    log_totals = row_max + jnp.log(row_sum)

    def mix_step(total, block, key_block, value_block, open_mask, own):
        weights_low = jnp.exp(block_scores(key_block, open_mask) - log_totals[..., None]).astype(
            jnp.bfloat16
        )
        return total + jnp.einsum(
            "hqk,khd->qhd", weights_low, value_block, preferred_element_type=jnp.float32
        )

    attended = sweep(mix_step, jnp.zeros((tokens, HEADS, HEAD_DIM), jnp.float32))
    attended_low = attended.reshape(tokens, D).astype(jnp.bfloat16)
    residual = inputs + product(attended_low, w_out)
    second_norm, second_inverse = norm_forward(residual, norm2_gain)
    second_low = second_norm.astype(jnp.bfloat16)
    gate_values = product(second_low, w_gate)
    up_values = product(second_low, w_up)
    sigmoid_gate = jax.nn.sigmoid(gate_values)
    activated = gate_values * sigmoid_gate
    hidden_low = (activated * up_values).astype(jnp.bfloat16)
    output = (residual + product(hidden_low, w_down)).astype(jnp.bfloat16)
    upstream = output_grad[0]
    grad_down = product_tn(hidden_low, upstream)
    grad_hidden = product_nt(upstream, w_down)
    grad_gate_low = (
        grad_hidden * up_values * sigmoid_gate * (1.0 + gate_values * (1.0 - sigmoid_gate))
    ).astype(jnp.bfloat16)
    grad_up_low = (grad_hidden * activated).astype(jnp.bfloat16)
    grad_gate = product_tn(second_low, grad_gate_low)
    grad_up = product_tn(second_low, grad_up_low)
    grad_second = product_nt(grad_gate_low, w_gate) + product_nt(grad_up_low, w_up)
    grad_residual, grad_norm2 = norm_backward(residual, second_inverse, norm2_gain, grad_second)
    grad_residual = grad_residual + upstream.astype(jnp.float32)
    residual_low = grad_residual.astype(jnp.bfloat16)
    grad_out = product_tn(attended_low, residual_low)
    grad_attended = product_nt(residual_low, w_out).astype(jnp.bfloat16)
    grad_heads = grad_attended.reshape(tokens, HEADS, HEAD_DIM)

    def probs_pair(key_block, value_block, open_mask):
        probs = jnp.exp(block_scores(key_block, open_mask) - log_totals[..., None])
        dprobs = jnp.einsum(
            "qhd,khd->hqk", grad_heads, value_block, preferred_element_type=jnp.float32
        )
        return (probs, dprobs)

    def delta_step(total, block, key_block, value_block, open_mask, own):
        probs, dprobs = probs_pair(key_block, value_block, open_mask)
        return total + jnp.sum(probs * dprobs, axis=2)

    delta_rows = sweep(delta_step, jnp.zeros((HEADS, tokens), jnp.float32))

    def grad_step(carry, block, key_block, value_block, open_mask, own):
        grad_query, key_terms, value_terms = carry
        probs, dprobs = probs_pair(key_block, value_block, open_mask)
        dscores = (probs * (dprobs - delta_rows[..., None])).astype(jnp.bfloat16)
        grad_query = grad_query + jnp.einsum(
            "hqk,khd->qhd", dscores, key_block, preferred_element_type=jnp.float32
        )
        if own:
            key_part = (
                jnp.einsum("hqk,qhd->khd", dscores, query_heads, preferred_element_type=jnp.float32)
                * score_scale
            )
            value_part = jnp.einsum(
                "hqk,qhd->khd",
                probs.astype(jnp.bfloat16),
                grad_heads,
                preferred_element_type=jnp.float32,
            )
            key_terms = lax.dynamic_update_index_in_dim(key_terms, key_part, block, 0)
            value_terms = lax.dynamic_update_index_in_dim(value_terms, value_part, block, 0)
        return (grad_query, key_terms, value_terms)

    term_shape = key_blocks.shape
    start_grads = (
        jnp.zeros((tokens, HEADS, HEAD_DIM), jnp.float32),
        jnp.zeros(term_shape, jnp.float32),
        jnp.zeros(term_shape, jnp.float32),
    )
    grad_query, key_terms, value_terms = sweep(grad_step, start_grads)
    grad_queries = (grad_query * score_scale).reshape(tokens, D)
    grad_keys, grad_values = (
        lax.psum_scatter(
            key_terms.astype(jnp.bfloat16), "seq", scatter_dimension=0, tiled=True
        ).astype(jnp.float32),
        lax.psum_scatter(
            value_terms.astype(jnp.bfloat16), "seq", scatter_dimension=0, tiled=True
        ).astype(jnp.float32),
    )
    grad_projected = jnp.concatenate(
        [
            rotate(grad_queries, cosine_table, sine_table, -1.0),
            rotate(grad_keys.reshape(tokens, D), cosine_table, sine_table, -1.0),
            grad_values.reshape(tokens, D),
        ],
        axis=1,
    ).astype(jnp.bfloat16)
    grad_qkv = product_tn(first_low, grad_projected)
    grad_first = product_nt(grad_projected, w_qkv)
    grad_inputs, grad_norm1 = norm_backward(inputs, first_inverse, norm1_gain, grad_first)
    input_grad = (grad_inputs + grad_residual)[None]
    shares = (
        lax.psum_scatter(
            grad_norm1.astype(jnp.bfloat16), "seq", scatter_dimension=0, tiled=True
        ).astype(jnp.float32),
        lax.psum_scatter(
            grad_norm2.astype(jnp.bfloat16), "seq", scatter_dimension=0, tiled=True
        ).astype(jnp.float32),
        lax.psum_scatter(
            grad_qkv.astype(jnp.bfloat16), "seq", scatter_dimension=0, tiled=True
        ).astype(jnp.float32),
        lax.psum_scatter(
            grad_out.astype(jnp.bfloat16), "seq", scatter_dimension=0, tiled=True
        ).astype(jnp.float32),
        lax.psum_scatter(
            grad_gate.astype(jnp.bfloat16), "seq", scatter_dimension=0, tiled=True
        ).astype(jnp.float32),
        lax.psum_scatter(
            grad_up.astype(jnp.bfloat16), "seq", scatter_dimension=0, tiled=True
        ).astype(jnp.float32),
        lax.psum_scatter(
            grad_down.astype(jnp.bfloat16), "seq", scatter_dimension=0, tiled=True
        ).astype(jnp.float32),
    )
    totals = (
        lax.psum(shares[0].astype(jnp.bfloat16), "seg").astype(jnp.float32),
        lax.psum(shares[1].astype(jnp.bfloat16), "seg").astype(jnp.float32),
        lax.psum(shares[2].astype(jnp.bfloat16), "seg").astype(jnp.float32),
        lax.psum(shares[3].astype(jnp.bfloat16), "seg").astype(jnp.float32),
        lax.psum(shares[4].astype(jnp.bfloat16), "seg").astype(jnp.float32),
        lax.psum(shares[5].astype(jnp.bfloat16), "seg").astype(jnp.float32),
        lax.psum(shares[6].astype(jnp.bfloat16), "seg").astype(jnp.float32),
    )
    return (
        output[None],
        input_grad,
        totals[0],
        totals[1],
        totals[2],
        totals[3],
        totals[4],
        totals[5],
        totals[6],
    )


def solution(mesh):
    placed = (
        P("seg", "seq", None),
        P("seg", "seq", None),
        P(),
        P(),
        P(),
        P(),
        P(),
        P(),
        P(),
        P("seg", "seq", None),
        P("seg", "seq", None),
        P(),
        P(),
    )
    return jax.shard_map(
        on_device,
        mesh=mesh,
        in_specs=placed,
        out_specs=(
            P("seg", "seq", None),
            P("seg", "seq", None),
            P("seq"),
            P("seq"),
            P("seq", None),
            P("seq", None),
            P("seq", None),
            P("seq", None),
            P("seq", None),
        ),
        check_vma=False,
    )
```

profile of v0, /device:TPU:0, one launch (start us, length us, event | category | flops | bytes accessed | tf_op | source)
XLA Modules:
  0.0 1502.4 jit_solution(4767216906355732668)
XLA Ops:
  10.8 6.0 fusion.176
  39.9 19.3 %all-gather.7.cloned.1.call-done = bf16[8,256,1024]{2,1,0:T(8,128)(2,1)} async-done(((bf16[1,256,1024]{2,1,0:T(8,128)(2,1)}), bf16[8,256,1024]{2,1,0:T(8,128)(2,1)}) %all-gather.7.cloned.1.call-update) | async-done | bytes 4194320 | tf_op jit(solution)/shard_map/all_gather | solution.py:85
  63.4 43.1 %all-gather.11.cloned.1.call-done = bf16[8,256,1024]{2,1,0:T(8,128)(2,1)} async-done(((bf16[1,256,1024]{2,1,0:T(8,128)(2,1)}), bf16[8,256,1024]{2,1,0:T(8,128)(2,1)}) %all-gather.11.cloned.1.call-update) | async-done | bytes 4194320 | tf_op jit(solution)/shard_map/all_gather | solution.py:84
  118.4 41.9 %all-gather.15.cloned.1.call-done = bf16[2048,1024]{1,0:T(8,128)(2,1)} async-done(((bf16[512,1024]{1,0:T(8,128)(2,1)}), bf16[2048,1024]{1,0:T(8,128)(2,1)}) %all-gather.15.cloned.1.call-update) | async-done | bytes 4194320 | tf_op jit(solution)/shard_map/all_gather | solution.py:106
  166.5 48.7 %all-gather.17.cloned.1.call-done = bf16[2048,1024]{1,0:T(8,128)(2,1)} async-done(((bf16[512,1024]{1,0:T(8,128)(2,1)}), bf16[2048,1024]{1,0:T(8,128)(2,1)}) %all-gather.17.cloned.1.call-update) | async-done | bytes 4194320 | tf_op jit(solution)/shard_map/all_gather | solution.py:107
  221.9 83.1 %all-gather.13.cloned.1.call-done = bf16[4,1024,1024]{2,1,0:T(8,128)(2,1)} async-done(((bf16[4,256,1024]{2,1,0:T(8,128)(2,1)}), bf16[4,1024,1024]{2,1,0:T(8,128)(2,1)}) %all-gather.13.cloned.1.call-update) | async-done | bytes 8388624 | tf_op jit(solution)/shard_map/all_gather | solution.py:90
  305.0 8.9 copy.127
  313.9 10.1 copy.87
  324.0 88.0 %while.112 = (s32[]{:T(128)}, f32[8,512]{1,0:T(8,128)S(1)}, f32[8,512]{1,0:T(8,128)S(1)}, bf16[8,512,8,128]{3,1,2,0:T(8,128)(2,1)}, bf16[512,8,128]{2,0,1:T(8,128)(2,1)S(1)}, /*index=5*/pred[]{:T(512)}, s32[]{:T(128)}, s32[]{:T(128)}) while((s32[]{:T(128)}, f32[8,512]{1,0:T(8,128)S(1)}, f32[8,512]{1,0:T(8,128)S(1)}, ...), condition=%wide.region_4.6_spmd.clone, body=%wide.region_1.5_spmd.clone.sunk | while | flops 551571456 | bytes 19088480 | solution.py:141
  324.4 5.8 fusion.292
  335.4 5.8 fusion.292
  346.3 5.8 fusion.292
  357.3 5.8 fusion.292
  368.2 5.8 fusion.292
  379.2 5.8 fusion.292
  390.1 5.8 fusion.292
  401.1 5.8 fusion.292
  416.8 8.9 copy.126
  425.7 9.1 copy.102
  434.8 85.3 %while.113 = (s32[]{:T(128)}, f32[512,8,128]{0,2,1:T(8,128)}, bf16[8,512,8,128]{3,2,1,0:T(8,128)(2,1)}, bf16[8,512,8,128]{3,1,2,0:T(8,128)(2,1)}, bf16[512,8,128...) while((s32[]{:T(128)}, f32[512,8,128]{0,2,1:T(8,128)}, ...), condition=%wide.region_10.12_spmd.clone, body=%wide.region_9.11_spmd.clone.sunk | while | flops 1083179008 | bytes 11551851 | solution.py:141
  449.7 6.1 bitcast_add_fusion.12
  460.4 6.1 bitcast_add_fusion.12
  471.2 6.1 bitcast_add_fusion.12
  481.9 6.1 bitcast_add_fusion.12
  492.6 6.1 bitcast_add_fusion.12
  503.4 6.1 bitcast_add_fusion.12
  514.1 6.1 bitcast_add_fusion.12
  520.2 11.2 while.109
  525.1 6.3 bitcast_add_fusion.10
  545.4 11.5 multiply_convert_fusion
  556.9 6.0 fusion.184
  569.2 48.3 %while.114 = (s32[]{:T(128)}, f32[8,512]{1,0:T(8,128)S(1)}, bf16[8,512,8,128]{3,1,2,0:T(8,128)(2,1)}, bf16[512,8,128]{2,0,1:T(8,128)(2,1)S(1)}, f32[8,512]{1,0:T...) while((s32[]{:T(128)}, f32[8,512]{1,0:T(8,128)S(1)}, ...), condition=%wide.region_17.19_spmd.clone, body=%wide.region_15.18_spmd.clone.sunk | while | flops 1084231680 | bytes 21055084 | solution.py:141
  618.5 13.1 while.110
  618.9 5.9 fusion.277
  625.0 6.5 fusion.278
  631.6 106.0 %while.115 = (s32[]{:T(128)}, f32[512,8,128]{0,2,1:T(8,128)S(1)}, bf16[8,512,8,128]{3,1,2,0:T(8,128)(2,1)}, bf16[512,8,128]{2,0,1:T(8,128)(2,1)S(1)}, f32[8,512]...) while((s32[]{:T(128)}, f32[512,8,128]{0,2,1:T(8,128)S(1)}, ...), condition=%wide.region_22.24_spmd.clone, body=%wide.region_21.23_spmd.clone.sunk | while | flops 1624244224 | bytes 26249336 | solution.py:141
  631.6 5.7 fusion.310
  637.3 7.5 bitcast_add_fusion.13
  650.6 7.5 bitcast_add_fusion.13
  663.8 7.5 bitcast_add_fusion.13
  677.1 7.5 bitcast_add_fusion.13
  690.3 7.5 bitcast_add_fusion.13
  703.6 7.5 bitcast_add_fusion.13
  716.8 7.5 bitcast_add_fusion.13
  730.1 7.5 bitcast_add_fusion.13
  743.4 22.3 %while.111 = (s32[]{:T(128)}, f32[512,8,128]{0,2,1:T(8,128)S(1)}, bf16[4,512,8,128]{3,1,2,0:T(8,128)(2,1)}, bf16[4,512,8,128]{3,1,2,0:T(8,128)(2,1)}, s32[]{:T(1...) while((s32[]{:T(128)}, f32[512,8,128]{0,2,1:T(8,128)S(1)}, ...), condition=%wide.region_24.26_spmd.clone, body=%wide.region_23.25_spmd.clone.sunk | while | flops 2706637824 | bytes 117236072 | solution.py:142
  743.6 5.8 fusion.289
  749.6 6.7 fusion.290
  771.5 7.8 convolution_convert_fusion.1
  780.6 6.8 convolution_convert_fusion.2
  788.6 6.9 convolution_convert_fusion
  802.1 168.8 %reduce-scatter.22.cloned.1.call-done = bf16[1,512,8,128]{3,1,2,0:T(8,128)(2,1)} async-done(((bf16[4,512,8,128]{3,1,2,0:T(8,128)(2,1)}), bf16[1,512,8,128]{3,1,2,0:T(8,128)(2,1)}) %reduce-scatter.22.cloned.1.call-update) | async-done | bytes 1048592
  978.9 47.6 %reduce-scatter.24.cloned.1.call-done = bf16[1,512,8,128]{3,1,2,0:T(8,128)(2,1)} async-done(((bf16[4,512,8,128]{3,1,2,0:T(8,128)(2,1)}), bf16[1,512,8,128]{3,1,2,0:T(8,128)(2,1)}) %reduce-scatter.24.cloned.1.call-update) | async-done | bytes 1048592
  1033.2 5.9 convolution_convert_fusion.3
  1039.4 25.3 %reduce-scatter.14.cloned.1.call-done = bf16[256,1024]{1,0:T(8,128)(2,1)} async-done(((bf16[1024,1024]{1,0:T(8,128)(2,1)}), bf16[256,1024]{1,0:T(8,128)(2,1)}) %reduce-scatter.14.cloned.1.call-update) | async-done | bytes 524304 | tf_op jit(solution)/shard_map/reduce_scatter | solution.py:266
  1064.7 68.5 %reduce-scatter.18.cloned.1.call-done = bf16[256,2816]{1,0:T(8,128)(2,1)} async-done(((bf16[1024,2816]{1,0:T(8,128)(2,1)}), bf16[256,2816]{1,0:T(8,128)(2,1)}) %reduce-scatter.18.cloned.1.call-update) | async-done | bytes 1441808 | tf_op jit(solution)/shard_map/reduce_scatter | solution.py:272
  1133.2 68.7 %reduce-scatter.16.cloned.1.call-done = bf16[256,2816]{1,0:T(8,128)(2,1)} async-done(((bf16[1024,2816]{1,0:T(8,128)(2,1)}), bf16[256,2816]{1,0:T(8,128)(2,1)}) %reduce-scatter.16.cloned.1.call-update) | async-done | bytes 1441808 | tf_op jit(solution)/shard_map/reduce_scatter | solution.py:269
  1201.9 68.5 %reduce-scatter.20.cloned.1.call-done = bf16[704,1024]{1,0:T(8,128)(2,1)} async-done(((bf16[2816,1024]{1,0:T(8,128)(2,1)}), bf16[704,1024]{1,0:T(8,128)(2,1)}) %reduce-scatter.20.cloned.1.call-update) | async-done | bytes 1441808 | tf_op jit(solution)/shard_map/reduce_scatter | solution.py:275
  1270.5 73.0 %reduce-scatter.12.cloned.1.call-done = bf16[256,3072]{1,0:T(8,128)(2,1)} async-done(((bf16[1024,3072]{1,0:T(8,128)(2,1)}), bf16[256,3072]{1,0:T(8,128)(2,1)}) %reduce-scatter.12.cloned.1.call-update) | async-done | bytes 1572880 | tf_op jit(solution)/shard_map/reduce_scatter | solution.py:263
  1345.5 7.8 fusion.166
  1353.3 8.1 fusion.157
  1361.4 8.9 all-reduce.6
  1370.4 15.4 %all-reduce.4 = (bf16[256]{0:T(256)(128)(2,1)S(1)}, bf16[256]{0:T(256)(128)(2,1)S(1)}) all-reduce(bf16[256]{0:T(256)(128)(2,1)S(1)} %dynamic-slice.5, bf16[256]{0:T(256)(128)(2,1)S(1)} %dynamic-slice.7), channel_id=1, replica_groups=mesh['seg'=8,'seq'=4] {'seg'}, use_global_device_ids=true, to_apply=%region_30.32 | all-reduce | flops 512 | bytes 2048 | tf_op jit(solution)/shard_map/psum | solution.py:280
  1390.5 94.6 %all-reduce.9.cloned.1.call-done = (bf16[256,3072]{1,0:T(8,128)(2,1)}, bf16[256,1024]{1,0:T(8,128)(2,1)}, bf16[256,2816]{1,0:T(8,128)(2,1)}, bf16[256,2816]{1,0:T(8,128)(2,1)}, bf16[704,1024]{1,0:T(8,128)(2,1)}) async-done(((bf16[256,3072]{1,0:T(8,128)(2,1)}, bf16[256,1024]{1,0:T(8,128)(2,1)}, bf16[256,2816]{1,0:T(8,128)(2,1)}, bf16[256,2816]{1,0:T(8,128)(2,1)}, bf16[704,1024]{1,0:T(8,128)(2,1)}), ...) | async-done | bytes 6422544 | tf_op jit(solution)/shard_map/psum | solution.py:282
  (320 shorter events, 323.4 us)
Async XLA Ops:
  7.2 526.1 %copy-start = (bf16[1024,1024]{1,0:T(8,128)(2,1)S(1)}, bf16[1024,1024]{1,0:T(8,128)(2,1)}, u32[]{:S(2)}) copy-start(bf16[1024,1024]{1,0:T(8,128)(2,1)} %param.36) | copy-start | bytes 6291460
  7.2 52.0 %all-gather.7.cloned.1.call-start = ((), (), s32[]{:S(2)}) async-start(), calls=%async_computation.7 | async-start | bytes 4718592 | tf_op jit(solution)/shard_map/all_gather | solution.py:85
  7.9 98.6 %all-gather.11.cloned.1.call-start = ((), (), s32[]{:S(2)}) async-start(), calls=%async_computation.9 | async-start | bytes 4718592 | tf_op jit(solution)/shard_map/all_gather | solution.py:84
  8.7 151.7 %all-gather.15.cloned.1.call-start = ((), (), s32[]{:S(2)}) async-start(), calls=%async_computation.11 | async-start | bytes 5242880 | tf_op jit(solution)/shard_map/all_gather | solution.py:106
  10.8 6.0 copy-start.43
  16.8 2.6 copy-start.11
  29.9 2.2 slice-start.2
  30.0 3.7 slice-start.3
  31.3 5.4 copy-start.7
  36.7 2.9 copy-start.46
  36.7 178.5 %all-gather.17.cloned.1.call-start = ((), (), s32[]{:S(2)}) async-start(), calls=%async_computation.12 | async-start | bytes 5242880 | tf_op jit(solution)/shard_map/all_gather | solution.py:107
  39.6 265.4 %all-gather.13.cloned.1.call-start = ((), (), s32[]{:S(2)}) async-start(), calls=%async_computation.10 | async-start | bytes 10485760 | tf_op jit(solution)/shard_map/all_gather | solution.py:90
  115.4 1.8 copy-start.48
  115.4 301.4 %all-gather.9.cloned.1.call-start = ((), (), s32[]{:S(2)}) async-start(), calls=%async_computation.8 | async-start | bytes 10485760 | tf_op jit(solution)/shard_map/all_gather | solution.py:91
  218.5 3.3 copy-start.3
  221.8 749.1 %reduce-scatter.22.cloned.1.call-start = ((), (), s32[]{:S(2)}) async-start(), calls=%async_computation.18 | async-start | bytes 5242880
  531.3 1.9 copy-start.12
  531.3 3.6 slice-start.4
  533.3 2.2 slice-start.5
  533.3 7.2 slice-start.6
  534.7 32.3 %copy-start.4 = (f32[512,1024]{1,0:T(8,128)}, f32[512,1024]{1,0:T(8,128)S(1)}, u32[]{:S(2)}) copy-start(f32[512,1024]{1,0:T(8,128)S(1)} %get-tuple-element.1348) | copy-start | bytes 6291460
  535.5 5.0 copy-start.32
  535.5 5.0 slice-start.7
  540.5 5.0 copy-start.28
  556.9 6.0 copy-start.50
  567.6 1.5 copy-start.22
  618.5 13.1 copy-start.2
  749.6 6.7 copy-start.9
  756.3 6.3 slice-start
  757.9 2.0 copy-start.10
  759.9 2.7 slice-start.1
  759.9 2.8 copy-start.35
  765.8 260.7 %reduce-scatter.24.cloned.1.call-start = ((), (), s32[]{:S(2)}) async-start(), calls=%async_computation.19 | async-start | bytes 5242880
  766.5 298.2 %reduce-scatter.14.cloned.1.call-start = ((), (), s32[]{:S(2)}) async-start(), calls=%async_computation.14 | async-start | bytes 2621440 | tf_op jit(solution)/shard_map/reduce_scatter | solution.py:266
  771.2 362.0 %reduce-scatter.18.cloned.1.call-start = ((), (), s32[]{:S(2)}) async-start(), calls=%async_computation.16 | async-start | bytes 7208960 | tf_op jit(solution)/shard_map/reduce_scatter | solution.py:272
  779.4 422.6 %reduce-scatter.16.cloned.1.call-start = ((), (), s32[]{:S(2)}) async-start(), calls=%async_computation.15 | async-start | bytes 7208960 | tf_op jit(solution)/shard_map/reduce_scatter | solution.py:269
  787.4 483.1 %reduce-scatter.20.cloned.1.call-start = ((), (), s32[]{:S(2)}) async-start(), calls=%async_computation.17 | async-start | bytes 7208960 | tf_op jit(solution)/shard_map/reduce_scatter | solution.py:275
  795.5 548.1 %reduce-scatter.12.cloned.1.call-start = ((), (), s32[]{:S(2)}) async-start(), calls=%async_computation.13 | async-start | bytes 7864320 | tf_op jit(solution)/shard_map/reduce_scatter | solution.py:263
  972.2 1.6 copy-start.6
  972.3 2.2 copy-start.17
  972.3 2.8 copy-start.18
  972.3 2.8 copy-start.26
  972.3 2.8 copy-start.27
  977.6 51.1 %copy-start.19 = (bf16[1,512,8,128]{3,1,2,0:T(8,128)(2,1)S(1)}, bf16[1,512,8,128]{3,1,2,0:T(8,128)(2,1)}, u32[]{:S(2)}) copy-start(bf16[1,512,8,128]{3,1,2,0:T(8,128)(2,1)} %reduce-scatter.22.cloned.1.call-done) | copy-start | bytes 3145732
  1028.4 2.0 copy-start.8
  1028.4 2.6 copy-start.16
  1028.7 3.5 copy-start.38
  1031.0 2.2 copy-start.13
  1031.0 2.2 copy-start.36
  1031.0 2.2 copy-start.44
  1031.0 2.2 copy-start.45
  1039.1 446.0 %all-reduce.9.cloned.1.call-start = ((), (), s32[]{:S(2)}) async-start(), calls=%async_computation.20 | async-start | bytes 12845056 | tf_op jit(solution)/shard_map/psum | solution.py:282
  1343.5 1.9 copy-start.5
  1345.4 7.8 copy-start.31
  1345.4 7.8 copy-start.37
  1345.5 7.8 copy-start.39
  1353.2 8.1 copy-start.47
  1353.3 33.7 %copy-start.15 = (f32[512,1024]{1,0:T(8,128)S(1)}, f32[512,1024]{1,0:T(8,128)}, u32[]{:S(2)}) copy-start(f32[512,1024]{1,0:T(8,128)} %copy-done.14) | copy-start | bytes 6291460
  1353.3 33.7 %copy-start.42 = (f32[512]{0:T(512)S(1)}, f32[512]{0:T(512)}, u32[]{:S(2)}) copy-start(f32[512]{0:T(512)} %get-tuple-element.1341) | copy-start | bytes 6148
  1485.1 3.6 copy-start.25
  1488.6 1.9 copy-start.24
  1490.4 1.9 copy-start.23
  1492.3 1.9 copy-start.40
  1492.3 3.0 copy-start.1
  (9 other events, 10.6 us)
Sparse Core Ops, SparseCore 0:
  9.6 49.5 all-gather.6
  60.8 45.6 all-gather.10
  109.0 51.3 all-gather.14
  162.6 52.5 all-gather.16
  217.5 87.4 all-gather.12
  307.3 87.4 all-gather.8
  765.9 204.9 reduce-scatter.21
  973.8 52.5 reduce-scatter.23
  1029.5 35.1 reduce-scatter.13
  1067.5 65.6 reduce-scatter.17
  1136.2 65.6 reduce-scatter.15
  1204.8 65.6 reduce-scatter.19
  1273.5 70.0 reduce-scatter.11
  1346.1 138.8 all-reduce.8
where the time goes:
time: 1510 us; the launch traced here: 1500 us
  waiting for transfers between devices  854 us (57%)
  matrix products  377 us (25%)
  local copies, waits for them, and re-layouts  138 us (9%)
  other arithmetic  89.1 us (6%)
  blocking collectives  24.3 us (2%)
  between operations  16.4 us (1%)
    unnamed x16, waiting for transfers between devices  219 us
    dot_general x27, matrix products, block_scores(): jnp.einsum('qhd,khd->hqk', query_heads, key_block, preferred_element_type...  127 us
    psum x1, waiting for transfers between devices, on_device(): lax.psum(shares[2].astype(jnp.bfloat16), 'seg').astype(jnp.float32)  94.6 us
    all_gather x1, waiting for transfers between devices, on_device(): lax.all_gather(chosen_keys, 'seq', axis=1, tiled=True)  83.1 us
    reduce_scatter x1, waiting for transfers between devices, on_device(): lax.psum_scatter(grad_qkv.astype(jnp.bfloat16), 'seq', scatter_dimension=...  73 us
    unnamed x123, local copies, waits for them, and re-layouts  69.1 us
    reduce_scatter x1, waiting for transfers between devices, on_device(): lax.psum_scatter(grad_gate.astype(jnp.bfloat16), 'seq', scatter_dimension...  68.7 us
    reduce_scatter x1, waiting for transfers between devices, on_device(): lax.psum_scatter(grad_down.astype(jnp.bfloat16), 'seq', scatter_dimension...  68.5 us
  transfers between devices with their start and end apart: 14, of which 13 were waited for; matrix products, arithmetic and copies ran while one was open for 16% of the time, Pallas kernels for 0%

commit v1 on v0

--- a/solution.py
+++ b/solution.py
@@ -9,6 +9,19 @@
 masked_score = -1e30
 epsilon = 1e-06
 rotary_base = 10000.0
+
+
+def gather_around(array, axis, dim):
+    ways = lax.axis_size(axis)
+    up = [(d, (d + 1) % ways) for d in range(ways)]
+    down = [(d, (d - 1) % ways) for d in range(ways)]
+    earlier, later = ([array], [array])
+    for _ in range(ways // 2):
+        earlier.append(lax.ppermute(earlier[-1], axis, up))
+    for _ in range((ways - 1) // 2):
+        later.append(lax.ppermute(later[-1], axis, down))
+    line = jnp.concatenate([*earlier[::-1], *later[1:]], axis=dim)
+    return jnp.roll(line, (lax.axis_index(axis) - ways // 2) * array.shape[dim], axis=dim)
 
 
 def product(former, latter):
@@ -81,7 +94,7 @@
     listed = lax.dynamic_index_in_dim(sources, seg_index, 0, keepdims=False)
     picked = jnp.concatenate([jnp.reshape(seg_index, (1,)), listed])
     every_keys, every_values = (
-        lax.all_gather(mem_keys, "seg", axis=0, tiled=True),
+        gather_around(mem_keys, "seg", 0),
         lax.all_gather(mem_values, "seg", axis=0, tiled=True),
     )
     chosen_keys = jnp.take(every_keys, picked, axis=0)

time: 1510 us -> 1480 us (0.980)
  waiting for transfers between devices: 854 us -> 790 us
    ppermute x0 -> x7, waiting for transfers between devices: none -> 56.1 us  [the longest x4 56.1 us: gather_around(): earlier.append(lax.ppermute(earlier[-1], axis, up))]
    all_gather x1 -> x0, waiting for transfers between devices: 43.1 us -> none  [on_device(): lax.all_gather(mem_keys, 'seg', axis=0, tiled=True)]
    all_gather x1, waiting for transfers between devices: 41.9 us -> 0.02 us  [on_device(): lax.all_gather(own_keys, 'seq', axis=0, tiled=True)]
    all_gather x1, waiting for transfers between devices: 19.3 us -> 0.01 us  [on_device(): lax.all_gather(mem_values, 'seg', axis=0, tiled=True)]
    all_gather x1, waiting for transfers between devices: 48.7 us -> 31.5 us  [on_device(): lax.all_gather(own_values, 'seq', axis=0, tiled=True)]
    unnamed x123 -> x142, local copies, waits for them, and re-layouts: 69.1 us -> 77.5 us
    unnamed x16 -> x15, waiting for transfers between devices: 219 us -> 218 us
  transfers between devices with their start and end apart: 14 -> 20, of which waited for: 13 -> 14; matrix products, arithmetic and copies ran while one was open for 16% -> 17% of each run, Pallas kernels for 0% -> 0%
where the time goes in v1:
time: 1480 us; the launch traced here: 1470 us
  waiting for transfers between devices  790 us (53%)
  matrix products  383 us (26%)
  local copies, waits for them, and re-layouts  149 us (10%)
  other arithmetic  89 us (6%)
  blocking collectives  24.4 us (2%)
  between operations  16.6 us (1%)
    unnamed x15, waiting for transfers between devices  218 us
    dot_general x27, matrix products, block_scores(): jnp.einsum('qhd,khd->hqk', query_heads, key_block, preferred_element_type...  128 us
    psum x1, waiting for transfers between devices, on_device(): lax.psum(shares[2].astype(jnp.bfloat16), 'seg').astype(jnp.float32)  95.2 us
    all_gather x1, waiting for transfers between devices, on_device(): lax.all_gather(chosen_keys, 'seq', axis=1, tiled=True)  83.1 us
    unnamed x142, local copies, waits for them, and re-layouts  77.5 us
    reduce_scatter x1, waiting for transfers between devices, on_device(): lax.psum_scatter(grad_qkv.astype(jnp.bfloat16), 'seq', scatter_dimension=...  72.9 us
    reduce_scatter x1, waiting for transfers between devices, on_device(): lax.psum_scatter(grad_up.astype(jnp.bfloat16), 'seq', scatter_dimension=0...  68.7 us
    reduce_scatter x1, waiting for transfers between devices, on_device(): lax.psum_scatter(grad_down.astype(jnp.bfloat16), 'seq', scatter_dimension...  68.7 us
  transfers between devices with their start and end apart: 20, of which 14 were waited for; matrix products, arithmetic and copies ran while one was open for 17% of the time, Pallas kernels for 0%

profile of v1, /device:TPU:0, one launch (start us, length us, event | category | flops | bytes accessed | tf_op | source)
XLA Modules:
  0.0 1465.9 jit_solution(4934068292817641301)
XLA Ops:
  10.7 6.0 fusion.176
  40.0 22.3 %collective-permute-done = bf16[1,256,1024]{2,1,0:T(8,128)(2,1)S(1)} collective-permute-done((bf16[1,256,1024]{2,1,0:T(8,128)(2,1)S(1)}, bf16[1,256,1024]{2,1,0:T(8,128)(2,1)S(1)}, u32[]{:S(2)}, u32[]{:S(2)}) %collective-permute-start) | collective-permute-done | bytes 524320 | tf_op jit(solution)/shard_map/ppermute | solution.py:20
  65.8 11.8 collective-permute-done.1
  81.1 11.9 collective-permute-done.2
  96.9 10.1 collective-permute-done.3
  142.2 31.5 %all-gather.14.cloned.1.call-done = bf16[2048,1024]{1,0:T(8,128)(2,1)} async-done(((bf16[512,1024]{1,0:T(8,128)(2,1)}), bf16[2048,1024]{1,0:T(8,128)(2,1)}) %all-gather.14.cloned.1.call-update) | async-done | bytes 4194320 | tf_op jit(solution)/shard_map/all_gather | solution.py:120
  180.4 83.1 %all-gather.10.cloned.1.call-done = bf16[4,1024,1024]{2,1,0:T(8,128)(2,1)} async-done(((bf16[4,256,1024]{2,1,0:T(8,128)(2,1)}), bf16[4,1024,1024]{2,1,0:T(8,128)(2,1)}) %all-gather.10.cloned.1.call-update) | async-done | bytes 8388624 | tf_op jit(solution)/shard_map/all_gather | solution.py:103
  263.5 8.9 copy.127
  272.4 10.2 copy.87
  282.5 87.7 %while.112 = (s32[]{:T(128)}, f32[8,512]{1,0:T(8,128)S(1)}, f32[8,512]{1,0:T(8,128)S(1)}, bf16[8,512,8,128]{3,1,2,0:T(8,128)(2,1)}, bf16[512,8,128]{2,0,1:T(8,128)(2,1)S(1)}, /*index=5*/pred[]{:T(512)}, s32[]{:T(128)}, s32[]{:T(128)}) while((s32[]{:T(128)}, f32[8,512]{1,0:T(8,128)S(1)}, f32[8,512]{1,0:T(8,128)S(1)}, ...), condition=%wide.region_4.6_spmd.clone, body=%wide.region_1.5_spmd.clone.sunk | while | flops 551571456 | bytes 19088480 | solution.py:154
  282.9 5.8 fusion.292
  293.8 5.8 fusion.292
  359.3 5.8 fusion.292
  375.0 8.9 copy.126
  383.9 9.0 copy.102
  392.9 85.3 %while.113 = (s32[]{:T(128)}, f32[512,8,128]{0,2,1:T(8,128)}, bf16[8,512,8,128]{3,2,1,0:T(8,128)(2,1)}, bf16[8,512,8,128]{3,1,2,0:T(8,128)(2,1)}, bf16[512,8,128...) while((s32[]{:T(128)}, f32[512,8,128]{0,2,1:T(8,128)}, ...), condition=%wide.region_10.12_spmd.clone, body=%wide.region_9.11_spmd.clone.sunk | while | flops 1083179008 | bytes 11551851 | solution.py:154
  407.8 6.1 bitcast_add_fusion.12
  418.6 6.1 bitcast_add_fusion.12
  429.3 6.1 bitcast_add_fusion.12
  440.0 6.1 bitcast_add_fusion.12
  450.8 6.1 bitcast_add_fusion.12
  461.5 6.1 bitcast_add_fusion.12
  472.2 6.1 bitcast_add_fusion.12
  478.3 11.2 while.109
  483.2 6.3 bitcast_add_fusion.10
  494.5 8.5 fusion.182
  508.0 12.0 multiply_convert_fusion
  531.5 48.3 %while.114 = (s32[]{:T(128)}, f32[8,512]{1,0:T(8,128)S(1)}, bf16[8,512,8,128]{3,1,2,0:T(8,128)(2,1)}, bf16[512,8,128]{2,0,1:T(8,128)(2,1)S(1)}, f32[8,512]{1,0:T...) while((s32[]{:T(128)}, f32[8,512]{1,0:T(8,128)S(1)}, ...), condition=%wide.region_17.19_spmd.clone, body=%wide.region_15.18_spmd.clone.sunk | while | flops 1084231680 | bytes 21055084 | solution.py:154
  580.7 13.1 while.110
  581.1 6.0 fusion.277
  587.4 6.5 fusion.278
  593.9 106.7 %while.115 = (s32[]{:T(128)}, f32[512,8,128]{0,2,1:T(8,128)S(1)}, bf16[8,512,8,128]{3,1,2,0:T(8,128)(2,1)}, bf16[512,8,128]{2,0,1:T(8,128)(2,1)S(1)}, f32[8,512]...) while((s32[]{:T(128)}, f32[512,8,128]{0,2,1:T(8,128)S(1)}, ...), condition=%wide.region_22.24_spmd.clone, body=%wide.region_21.23_spmd.clone.sunk | while | flops 1624244224 | bytes 26249336 | solution.py:154
  599.7 7.5 bitcast_add_fusion.13
  613.1 7.5 bitcast_add_fusion.13
  620.6 5.8 fusion.310
  626.4 7.5 bitcast_add_fusion.13
  633.9 5.8 fusion.310
  639.7 7.5 bitcast_add_fusion.13
  647.3 5.8 fusion.310
  653.1 7.5 bitcast_add_fusion.13
  666.4 7.5 bitcast_add_fusion.13
  673.9 5.8 fusion.310
  679.8 7.5 bitcast_add_fusion.13
  687.3 5.8 fusion.310
  693.1 7.5 bitcast_add_fusion.13
  706.5 22.4 %while.111 = (s32[]{:T(128)}, f32[512,8,128]{0,2,1:T(8,128)S(1)}, bf16[4,512,8,128]{3,1,2,0:T(8,128)(2,1)}, bf16[4,512,8,128]{3,1,2,0:T(8,128)(2,1)}, s32[]{:T(1...) while((s32[]{:T(128)}, f32[512,8,128]{0,2,1:T(8,128)S(1)}, ...), condition=%wide.region_24.26_spmd.clone, body=%wide.region_23.25_spmd.clone.sunk | while | flops 2706637824 | bytes 117236072 | solution.py:155
  706.6 5.8 fusion.289
  712.7 6.7 fusion.290
  734.6 7.9 convolution_convert_fusion.1
  743.7 6.8 convolution_convert_fusion.2
  751.7 6.9 convolution_convert_fusion
  765.2 169.3 %reduce-scatter.22.cloned.1.call-done = bf16[1,512,8,128]{3,1,2,0:T(8,128)(2,1)} async-done(((bf16[4,512,8,128]{3,1,2,0:T(8,128)(2,1)}), bf16[1,512,8,128]{3,1,2,0:T(8,128)(2,1)}) %reduce-scatter.22.cloned.1.call-update) | async-done | bytes 1048592
  942.5 47.6 %reduce-scatter.24.cloned.1.call-done = bf16[1,512,8,128]{3,1,2,0:T(8,128)(2,1)} async-done(((bf16[4,512,8,128]{3,1,2,0:T(8,128)(2,1)}), bf16[1,512,8,128]{3,1,2,0:T(8,128)(2,1)}) %reduce-scatter.24.cloned.1.call-update) | async-done | bytes 1048592
  995.3 5.9 convolution_convert_fusion.3
  1001.6 26.7 %reduce-scatter.14.cloned.1.call-done = bf16[256,1024]{1,0:T(8,128)(2,1)} async-done(((bf16[1024,1024]{1,0:T(8,128)(2,1)}), bf16[256,1024]{1,0:T(8,128)(2,1)}) %reduce-scatter.14.cloned.1.call-update) | async-done | bytes 524304 | tf_op jit(solution)/shard_map/reduce_scatter | solution.py:279
  1028.3 68.7 %reduce-scatter.18.cloned.1.call-done = bf16[256,2816]{1,0:T(8,128)(2,1)} async-done(((bf16[1024,2816]{1,0:T(8,128)(2,1)}), bf16[256,2816]{1,0:T(8,128)(2,1)}) %reduce-scatter.18.cloned.1.call-update) | async-done | bytes 1441808 | tf_op jit(solution)/shard_map/reduce_scatter | solution.py:285
  1097.0 68.5 %reduce-scatter.16.cloned.1.call-done = bf16[256,2816]{1,0:T(8,128)(2,1)} async-done(((bf16[1024,2816]{1,0:T(8,128)(2,1)}), bf16[256,2816]{1,0:T(8,128)(2,1)}) %reduce-scatter.16.cloned.1.call-update) | async-done | bytes 1441808 | tf_op jit(solution)/shard_map/reduce_scatter | solution.py:282
  1165.5 68.7 %reduce-scatter.20.cloned.1.call-done = bf16[704,1024]{1,0:T(8,128)(2,1)} async-done(((bf16[2816,1024]{1,0:T(8,128)(2,1)}), bf16[704,1024]{1,0:T(8,128)(2,1)}) %reduce-scatter.20.cloned.1.call-update) | async-done | bytes 1441808 | tf_op jit(solution)/shard_map/reduce_scatter | solution.py:288
  1234.2 72.9 %reduce-scatter.12.cloned.1.call-done = bf16[256,3072]{1,0:T(8,128)(2,1)} async-done(((bf16[1024,3072]{1,0:T(8,128)(2,1)}), bf16[256,3072]{1,0:T(8,128)(2,1)}) %reduce-scatter.12.cloned.1.call-update) | async-done | bytes 1572880 | tf_op jit(solution)/shard_map/reduce_scatter | solution.py:276
  1308.4 7.8 fusion.166
  1316.2 8.1 fusion.157
  1324.3 9.1 all-reduce.6
  1333.6 15.3 %all-reduce.4 = (bf16[256]{0:T(256)(128)(2,1)S(1)}, bf16[256]{0:T(256)(128)(2,1)S(1)}) all-reduce(bf16[256]{0:T(256)(128)(2,1)S(1)} %dynamic-slice.5, bf16[256]{0:T(256)(128)(2,1)S(1)} %dynamic-slice.7), channel_id=1, replica_groups=mesh['seg'=8,'seq'=4] {'seg'}, use_global_device_ids=true, to_apply=%region_30.32 | all-reduce | flops 512 | bytes 2048 | tf_op jit(solution)/shard_map/psum | solution.py:293
  1353.5 95.2 %all-reduce.9.cloned.1.call-done = (bf16[256,3072]{1,0:T(8,128)(2,1)}, bf16[256,1024]{1,0:T(8,128)(2,1)}, bf16[256,2816]{1,0:T(8,128)(2,1)}, bf16[256,2816]{1,0:T(8,128)(2,1)}, bf16[704,1024]{1,0:T(8,128)(2,1)}) async-done(((bf16[256,3072]{1,0:T(8,128)(2,1)}, bf16[256,1024]{1,0:T(8,128)(2,1)}, bf16[256,2816]{1,0:T(8,128)(2,1)}, bf16[256,2816]{1,0:T(8,128)(2,1)}, bf16[704,1024]{1,0:T(8,128)(2,1)}), ...) | async-done | bytes 6422544 | tf_op jit(solution)/shard_map/psum | solution.py:295
  (352 shorter events, 352.4 us)
Async XLA Ops:
  7.2 484.0 %copy-start = (bf16[1024,1024]{1,0:T(8,128)(2,1)S(1)}, bf16[1024,1024]{1,0:T(8,128)(2,1)}, u32[]{:S(2)}) copy-start(bf16[1024,1024]{1,0:T(8,128)(2,1)} %param.36) | copy-start | bytes 6291460
  7.2 116.6 %all-gather.6.cloned.1.call-start = ((), (), s32[]{:S(2)}) async-start(), calls=%async_computation.7 | async-start | bytes 4718592 | tf_op jit(solution)/shard_map/all_gather | solution.py:98
  7.9 128.1 %all-gather.12.cloned.1.call-start = ((), (), s32[]{:S(2)}) async-start(), calls=%async_computation.10 | async-start | bytes 5242880 | tf_op jit(solution)/shard_map/all_gather | solution.py:119
  16.7 2.6 copy-start.11
  29.8 2.2 slice-start.2
  29.8 3.7 slice-start.3
  31.1 5.4 copy-start.7
  36.5 3.0 copy-start.21
  36.5 56.6 %copy-start.48 = (s32[8,3]{0,1:T(4,128)S(1)}, s32[8,3]{0,1:T(4,128)}, u32[]{:S(2)}) copy-start(s32[8,3]{0,1:T(4,128)} %param.43) | copy-start | bytes 292
  36.5 137.2 %all-gather.14.cloned.1.call-start = ((), (), s32[]{:S(2)}) async-start(), calls=%async_computation.11 | async-start | bytes 5242880 | tf_op jit(solution)/shard_map/all_gather | solution.py:120
  39.4 224.1 %all-gather.10.cloned.1.call-start = ((), (), s32[]{:S(2)}) async-start(), calls=%async_computation.9 | async-start | bytes 10485760 | tf_op jit(solution)/shard_map/all_gather | solution.py:103
  39.5 22.8 %collective-permute-start = (bf16[1,256,1024]{2,1,0:T(8,128)(2,1)S(1)}, bf16[1,256,1024]{2,1,0:T(8,128)(2,1)S(1)}, u32[]{:S(2)}, u32[]{:S(2)}) collective-permute-start(bf16[1,256,1024]{2,1,0:T(8,128)(2,1)S(1)} %copy-done.21), channel_id=1, source_target_pairs={{0,4},{4,8},{8,12},{12,16},{16,20},{20,24},{24,28},{28,0},{1,5},{5... | collective-permute-start | bytes 1572872 | tf_op jit(solution)/shard_map/ppermute | solution.py:20
  62.2 15.3 %collective-permute-start.1 = (bf16[1,256,1024]{2,1,0:T(8,128)(2,1)S(1)}, bf16[1,256,1024]{2,1,0:T(8,128)(2,1)S(1)}, u32[]{:S(2)}, u32[]{:S(2)}) collective-permute-start(bf16[1,256,1024]{2,1,0:T(8,128)(2,1)S(1)} %collective-permute-done), channel_id=1, source_target_pairs={{0,4},{4,8},{8,12},{12,16},{16,20},{20,24},{24,28},{28,0},{1,5},{5... | collective-permute-start | bytes 1572872 | tf_op jit(solution)/shard_map/ppermute | solution.py:20
  62.2 15.3 %collective-permute-start.4 = (bf16[1,256,1024]{2,1,0:T(8,128)(2,1)S(1)}, bf16[1,256,1024]{2,1,0:T(8,128)(2,1)}, u32[]{:S(2)}, u32[]{:S(2)}) collective-permute-start(bf16[1,256,1024]{2,1,0:T(8,128)(2,1)S(1)} %copy-done.21), channel_id=1, source_target_pairs={{0,28},{4,0},{8,4},{12,8},{16,12},{20,16},{24,20},{28,24},{1,29},{... | collective-permute-start | bytes 1572872 | tf_op jit(solution)/shard_map/ppermute | solution.py:22
  77.6 15.5 %collective-permute-start.2 = (bf16[1,256,1024]{2,1,0:T(8,128)(2,1)S(1)}, bf16[1,256,1024]{2,1,0:T(8,128)(2,1)}, u32[]{:S(2)}, u32[]{:S(2)}) collective-permute-start(bf16[1,256,1024]{2,1,0:T(8,128)(2,1)S(1)} %collective-permute-done.1), channel_id=1, source_target_pairs={{0,4},{4,8},{8,12},{12,16},{16,20},{20,24},{24,28},{28,0},{1,5},{5... | collective-permute-start | bytes 1572872 | tf_op jit(solution)/shard_map/ppermute | solution.py:20
  78.4 15.0 %collective-permute-start.5 = (bf16[1,256,1024]{2,1,0:T(8,128)(2,1)}, bf16[1,256,1024]{2,1,0:T(8,128)(2,1)}, u32[]{:S(2)}, u32[]{:S(2)}) collective-permute-start(bf16[1,256,1024]{2,1,0:T(8,128)(2,1)} %collective-permute-done.4), channel_id=1, source_target_pairs={{0,28},{4,0},{8,4},{12,8},{16,12},{20,16},{24,20},{28,24},{1,29},{... | collective-permute-start | bytes 1572872 | tf_op jit(solution)/shard_map/ppermute | solution.py:22
  93.1 14.0 collective-permute-start.3
  93.4 19.3 %collective-permute-start.6 = (bf16[1,256,1024]{2,1,0:T(8,128)(2,1)}, bf16[1,256,1024]{2,1,0:T(8,128)(2,1)S(1)}, u32[]{:S(2)}, u32[]{:S(2)}) collective-permute-start(bf16[1,256,1024]{2,1,0:T(8,128)(2,1)} %collective-permute-done.5), channel_id=1, source_target_pairs={{0,28},{4,0},{8,4},{12,8},{16,12},{20,16},{24,20},{28,24},{1,29},{... | collective-permute-start | bytes 1572872 | tf_op jit(solution)/shard_map/ppermute | solution.py:22
  109.2 5.6 copy-start.23
  133.1 242.0 %all-gather.8.cloned.1.call-start = ((), (), s32[]{:S(2)}) async-start(), calls=%async_computation.8 | async-start | bytes 10485760 | tf_op jit(solution)/shard_map/all_gather | solution.py:104
  177.0 3.3 copy-start.3
  180.3 754.2 %reduce-scatter.22.cloned.1.call-start = ((), (), s32[]{:S(2)}) async-start(), calls=%async_computation.17 | async-start | bytes 5242880
  489.4 4.8 copy-start.43
  491.2 3.3 copy-start.19
  491.2 11.8 slice-start.6
  494.2 35.1 %copy-start.4 = (f32[512,1024]{1,0:T(8,128)}, f32[512,1024]{1,0:T(8,128)S(1)}, u32[]{:S(2)}) copy-start(f32[512,1024]{1,0:T(8,128)S(1)} %get-tuple-element.1348) | copy-start | bytes 6291460
  494.5 8.5 copy-start.34
  494.5 8.5 slice-start.7
  503.0 5.0 copy-start.30
  503.0 17.0 %slice-start.4 = ((s8[5767168]{0:T(1024)(128)(4,1)}), s8[4194304]{0:T(1024)(128)(4,1)S(1)}, s32[]{:S(2)}) async-start(s8[5767168]{0:T(1024)(128)(4,1)} %bitcast.439), calls=%async_computation.24 | async-start | bytes 8388608
  508.0 12.0 slice-start.5
  520.1 5.1 copy-start.52
  580.7 13.2 copy-start.2
  712.7 6.7 copy-start.9
  719.4 6.3 slice-start
  723.0 2.7 slice-start.1
  723.0 2.8 copy-start.37
  728.9 261.2 %reduce-scatter.24.cloned.1.call-start = ((), (), s32[]{:S(2)}) async-start(), calls=%async_computation.18 | async-start | bytes 5242880
  729.6 298.6 %reduce-scatter.14.cloned.1.call-start = ((), (), s32[]{:S(2)}) async-start(), calls=%async_computation.13 | async-start | bytes 2621440 | tf_op jit(solution)/shard_map/reduce_scatter | solution.py:279
  734.3 362.6 %reduce-scatter.18.cloned.1.call-start = ((), (), s32[]{:S(2)}) async-start(), calls=%async_computation.15 | async-start | bytes 7208960 | tf_op jit(solution)/shard_map/reduce_scatter | solution.py:285
  742.5 423.0 %reduce-scatter.16.cloned.1.call-start = ((), (), s32[]{:S(2)}) async-start(), calls=%async_computation.14 | async-start | bytes 7208960 | tf_op jit(solution)/shard_map/reduce_scatter | solution.py:282
  750.5 483.7 %reduce-scatter.20.cloned.1.call-start = ((), (), s32[]{:S(2)}) async-start(), calls=%async_computation.16 | async-start | bytes 7208960 | tf_op jit(solution)/shard_map/reduce_scatter | solution.py:288
  758.6 548.5 %reduce-scatter.12.cloned.1.call-start = ((), (), s32[]{:S(2)}) async-start(), calls=%async_computation.12 | async-start | bytes 7864320 | tf_op jit(solution)/shard_map/reduce_scatter | solution.py:276
  935.9 2.8 copy-start.17
  935.9 2.8 copy-start.28
  935.9 2.8 copy-start.29
  941.2 51.2 %copy-start.18 = (bf16[1,512,8,128]{3,1,2,0:T(8,128)(2,1)S(1)}, bf16[1,512,8,128]{3,1,2,0:T(8,128)(2,1)}, u32[]{:S(2)}) copy-start(bf16[1,512,8,128]{3,1,2,0:T(8,128)(2,1)} %reduce-scatter.22.cloned.1.call-done) | copy-start | bytes 3145732
  942.5 50.6 %copy-start.8 = (f32[512,8,128]{2,1,0:T(8,128)S(1)}, f32[512,8,128]{2,1,0:T(8,128)}, u32[]{:S(2)}) copy-start(f32[512,8,128]{2,1,0:T(8,128)} %copy-done.7) | copy-start | bytes 6291460
  990.1 3.0 copy-start.15
  993.1 2.2 copy-start.12
  1001.2 305.9 %copy-start.51 = (u32[32]{0:T(128)S(1)}, u32[32]{0:T(128)}, u32[]{:S(2)}) copy-start(u32[32]{0:T(128)} %constant.308) | copy-start | bytes 388
  1001.3 307.1 %copy-start.5 = (f32[512,1024]{1,0:T(8,128)S(1)}, f32[512,1024]{1,0:T(8,128)}, u32[]{:S(2)}) copy-start(f32[512,1024]{1,0:T(8,128)} %copy-done.4) | copy-start | bytes 6291460
  1001.3 447.5 %all-reduce.9.cloned.1.call-start = ((), (), s32[]{:S(2)}) async-start(), calls=%async_computation.19 | async-start | bytes 12845056 | tf_op jit(solution)/shard_map/psum | solution.py:295
  1308.4 7.8 copy-start.33
  1308.4 7.8 copy-start.39
  1308.4 7.8 copy-start.41
  1316.2 8.1 copy-start.49
  1316.2 33.9 %copy-start.14 = (f32[512,1024]{1,0:T(8,128)S(1)}, f32[512,1024]{1,0:T(8,128)}, u32[]{:S(2)}) copy-start(f32[512,1024]{1,0:T(8,128)} %copy-done.13) | copy-start | bytes 6291460
  1316.2 33.8 %copy-start.44 = (f32[512]{0:T(512)S(1)}, f32[512]{0:T(512)}, u32[]{:S(2)}) copy-start(f32[512]{0:T(512)} %get-tuple-element.1341) | copy-start | bytes 6148
  1448.8 3.6 copy-start.27
  1448.8 5.4 copy-start.26
  1452.3 3.5 copy-start.25
  1454.1 4.8 copy-start.1
  1454.1 3.7 copy-start.42
  (17 other events, 26.2 us)
Sparse Core Ops, SparseCore 0:
  9.6 55.1 all-gather.5
  67.3 51.3 all-gather.11
  121.1 52.5 all-gather.13
  176.0 87.4 all-gather.9
  265.7 87.4 all-gather.7
  729.0 205.4 reduce-scatter.21
  937.4 52.5 reduce-scatter.23
  993.0 35.1 reduce-scatter.13
  1031.3 65.6 reduce-scatter.17
  1099.8 65.6 reduce-scatter.15
  1168.5 65.6 reduce-scatter.19
  1237.0 70.0 reduce-scatter.11
  1309.8 138.8 all-reduce.8
